TPU v7x, 512 devices: a whole 4x4x16 slice. The times are simulated.
512 devices in a mesh: tm: 16 (over y, z_lo), sx: 8 (over z_hi, core), sy: 4 (over x).
Axes of the slice: x: 4, y: 4, z: 16 (z_hi: 4, z_lo: 4; z = z_hi * 4 + z_lo), core: 2. Of those that a mesh axis runs over, the one named last changes fastest.
Arguments:
- initial: float32 [8, 4, 5, 64, 128], P('sx', 'sy'), may hold values from -6 to 6
- viscosity: float32 [8, 4, 128], P('sx', 'sy'), may hold values from 0.5 to 5
- flux_jacobian: float32 [3, 5, 5], replicated, may hold values from -2 to 2
Outputs:
- nodes: float32 [16, 3, 8, 4, 5, 64, 128], P('tm', None, 'sx', 'sy')
All inputs are finite; a program needn't handle non-finite values.
Results may differ from a plain program's by a relative error of at most 0.0001.
Values sent between devices are 32-bit elements; how exact they have to be, the bound alone decides.
A program may use at most 64 MiB of HBM per device.

v0:
```python
import math

import jax
import jax.numpy as jnp
from jax import lax
from jax.sharding import PartitionSpec as P

ITERS = 2
JF = 3
JC = 2


SIGMA = 3.0
BETA = 0.5
STEP = 0.1
HALF_STEP = 0.05
TWO_THIRDS = 2.0 / 3.0
ONE_THIRD = 1.0 / 3.0
HIGHEST = lax.Precision.HIGHEST
WEIGHTS = ((5.0 / 24.0, 1.0 / 3.0, -1.0 / 24.0), (-1.0 / 24.0, 1.0 / 3.0, 5.0 / 24.0))


def passed_along(block, axis, distance):
    devices = range(lax.axis_size(axis))
    route = [(i - distance, i) for i in devices if i - distance in devices]
    return lax.ppermute(block, axis, route)


def kron_three(first, second, third):
    return jnp.kron(jnp.kron(first, second), third)


def node_tables():
    places = jnp.arange(4)
    row = places[:, None]
    column = places[None, :]
    identity = (row == column).astype(jnp.float32)
    upper = (row + 1 == column).astype(jnp.float32)
    border = identity * ((row == 0) | (row == 3)).astype(jnp.float32)
    line_laplace = 2.0 * identity - upper - upper.T - border
    line_grad = 0.5 * upper - 0.5 * upper.T
    laplace = (
        kron_three(line_laplace, identity, identity)
        + kron_three(identity, line_laplace, identity)
        + kron_three(identity, identity, line_laplace)
        + SIGMA * jnp.eye(64, dtype=jnp.float32)
    )
    grads = jnp.stack(
        [
            kron_three(line_grad, identity, identity),
            kron_three(identity, line_grad, identity),
            kron_three(identity, identity, line_grad),
        ]
    )
    weighting = jnp.where(row == 0, 0.5, math.sqrt(0.5)).astype(jnp.float32)
    cosine = weighting * jnp.cos(
        math.pi * row.astype(jnp.float32) * (2.0 * column.astype(jnp.float32) + 1.0) / 8.0
    )
    basis = kron_three(cosine, cosine, cosine)
    line_eigen = 2.0 - 2.0 * jnp.cos(math.pi * places.astype(jnp.float32) / 4.0)
    spectrum = (
        line_eigen[:, None, None] + line_eigen[None, :, None] + line_eigen[None, None, :]
    ).reshape(64) + SIGMA
    return (laplace, grads, basis, spectrum)


def previous(array, axis):
    widths = [(0, 0)] * array.ndim
    widths[axis] = (1, 0)
    return lax.slice_in_dim(jnp.pad(array, widths), 0, array.shape[axis], axis=axis)


def following(array, axis):
    widths = [(0, 0)] * array.ndim
    widths[axis] = (0, 1)
    return lax.slice_in_dim(jnp.pad(array, widths), 1, array.shape[axis] + 1, axis=axis)


def place(before, after, axis):
    empty = jnp.zeros_like(before)
    return jnp.stack([before, empty, empty, after], axis=axis)


def neighbours(field):
    lattice = field.reshape(field.shape[:4] + (4, 4, 4) + field.shape[-1:])
    high_x = lattice[:, :, :, :, 3]
    low_x = lattice[:, :, :, :, 0]
    from_west = passed_along(high_x[:, -1], "sx", 1)
    from_east = passed_along(low_x[:, 0], "sx", -1)
    before_x = jnp.concatenate([from_west[:, None], high_x[:, :-1]], axis=1)
    after_x = jnp.concatenate([low_x[:, 1:], from_east[:, None]], axis=1)
    high_y = lattice[:, :, :, :, :, 3]
    low_y = lattice[:, :, :, :, :, 0]
    from_south = passed_along(high_y[:, :, -1], "sy", 1)
    from_north = passed_along(low_y[:, :, 0], "sy", -1)
    before_y = jnp.concatenate([from_south[:, :, None], high_y[:, :, :-1]], axis=2)
    after_y = jnp.concatenate([low_y[:, :, 1:], from_north[:, :, None]], axis=2)
    along_x = place(before_x, after_x, 4)
    along_y = place(before_y, after_y, 5)
    along_z = place(previous(lattice[..., 3, :], 6), following(lattice[..., 0, :], 6), 6)
    return (along_x + along_y + along_z).reshape(field.shape)


def apply_operator(field, coeff, flux_jacobian, laplace, grads, coupled):
    volume = jnp.einsum("mn,bxyfnz->bxyfmz", laplace, field, precision=HIGHEST)
    slopes = jnp.einsum("dmn,bxyfnz->dbxyfmz", grads, field, precision=HIGHEST)
    transport = jnp.einsum("dgf,dbxyfmz->bxygmz", flux_jacobian, slopes, precision=HIGHEST)
    return coeff * (volume - BETA * coupled) + transport


def precondition(residue, coeff, basis, spectrum, step):
    inverse = 1.0 / (1.0 + step * coeff * spectrum[:, None])
    modes = jnp.einsum("kn,bxyfnz->bxyfkz", basis, residue, precision=HIGHEST)
    return jnp.einsum("kn,bxyfkz->bxyfnz", basis, modes * inverse, precision=HIGHEST)


def block_jacobi(target, begin, force, step, turns, operate, solve):
    field = begin
    image = -force
    for turn in range(turns):
        if turn > 0:
            image = operate(field)
        field = field + solve(target - field - step * image, step)
    return field


def local(initial, viscosity, flux_jacobian):
    laplace, grads, basis, spectrum = node_tables()
    coeff = viscosity[None, :, :, None, None, :]
    first_slice = lax.axis_index("tm") == 0

    def operate(field):
        return apply_operator(field, coeff, flux_jacobian, laplace, grads, neighbours(field))

    def solve(residue, step):
        return precondition(residue, coeff, basis, spectrum, step)

    start = initial[None]
    force_zero = -operate(start)
    values = [start, start, start]
    forces = [force_zero, force_zero, force_zero]
    for sweep in range(ITERS):
        old = list(forces)
        for node in range(2):
            weight = WEIGHTS[node]
            integral = STEP * (weight[0] * old[0] + weight[1] * old[1] + weight[2] * old[2])
            target = values[node] - HALF_STEP * old[node + 1] + integral
            values[node + 1] = block_jacobi(
                target, values[node + 1], old[node + 1], HALF_STEP, JF, operate, solve
            )
            forces[node + 1] = -operate(values[node + 1])
        correction = STEP * (TWO_THIRDS * forces[1] - ONE_THIRD * forces[0] - ONE_THIRD * forces[2])
        offset = -STEP * forces[2] + HALF_STEP * (forces[0] + forces[2]) + correction
        end_value = values[2]
        end_force = forces[2]

        def chain_turn(turn, carry):
            coarse_start, coarse_end = carry
            coarse_end = block_jacobi(
                coarse_start + offset, end_value, end_force, STEP, JC, operate, solve
            )
            passed = passed_along(coarse_end, "tm", 1)
            return (jnp.where(first_slice, start, passed), coarse_end)

        coarse_start, coarse_end = lax.fori_loop(0, lax.axis_size("tm"), chain_turn, (start, start))
        if sweep + 1 < ITERS:
            both = -operate(jnp.concatenate([coarse_start, coarse_end], axis=0))
            force_start = both[:1]
            force_end = both[1:]
            delta_start = force_start - forces[0]
            delta_end = force_end - forces[2]
            forces = [
                forces[0] + delta_start,
                forces[1] + 0.5 * (delta_start + delta_end),
                forces[2] + delta_end,
            ]
        move_start = coarse_start - values[0]
        move_end = coarse_end - values[2]
        values = [
            values[0] + move_start,
            values[1] + 0.5 * (move_start + move_end),
            values[2] + move_end,
        ]
    return jnp.stack(values, axis=1)


def solution(mesh):
    return jax.shard_map(
        local,
        mesh=mesh,
        in_specs=(P("sx", "sy", None, None, None), P("sx", "sy", None), P()),
        out_specs=P("tm", None, "sx", "sy", None, None, None),
        check_vma=False,
    )
```

profile of v0, /device:TPU:9, one launch (start us, length us, event | category | flops | bytes accessed | tf_op | source)
XLA Modules:
  0.0 1198.2 jit_solution(11969017696326933794)
XLA Ops:
  8.6 9.0 collective-permute-start.10
  44.9 9.6 collective-permute-start.18
  68.4 9.0 collective-permute-start.22
  89.7 9.0 collective-permute-start.26
  103.7 7.8 collective-permute-start.34
  122.0 7.8 collective-permute-start.30
  141.7 459.9 %while.32 = (s32[]{:T(128)}, f32[1,1,1,5,64,128]{5,4,3,2,1,0:T(8,128)S(1)}, f32[1,1,1,5,64,128]{5,4,3,2,1,0:T(8,128)}, pred[]{:T(512)}, f32[1,1,1,5,64,128]{5,4,...) while((s32[]{:T(128)}, ...), condition=%wide.region_1.2_spmd.clone.clone, body=%wide.region_0.1_spmd.clone.clone.sunk | while | flops 260067584 | bytes 8477726 | solution.py:165
  145.3 9.0 collective-permute-start.1
  175.3 7.5 collective-permute-start.1
  193.6 6.8 collective-permute-done.4
  204.0 7.5 collective-permute-start.1
  232.6 7.5 collective-permute-start.1
  250.8 7.3 collective-permute-done.4
  261.7 7.5 collective-permute-start.1
  290.3 7.5 collective-permute-start.1
  318.9 7.5 collective-permute-start.1
  347.5 7.5 collective-permute-start.1
  376.2 7.5 collective-permute-start.1
  404.8 7.5 collective-permute-start.1
  433.4 7.5 collective-permute-start.1
  462.0 7.5 collective-permute-start.1
  490.6 7.5 collective-permute-start.1
  519.3 7.5 collective-permute-start.1
  547.9 7.5 collective-permute-start.1
  576.5 7.5 collective-permute-start.1
  621.1 9.0 collective-permute-start.42
  642.1 9.0 collective-permute-start.46
  664.5 8.9 collective-permute-start.50
  685.3 8.1 collective-permute-start.54
  698.5 7.8 collective-permute-start.62
  716.9 7.8 collective-permute-start.58
  736.7 459.5 %while.33 = (s32[]{:T(128)}, f32[1,1,1,5,64,128]{5,4,3,2,1,0:T(8,128)S(1)}, f32[1,1,1,5,64,128]{5,4,3,2,1,0:T(8,128)}, pred[]{:T(512)}, f32[1,1,1,5,64,128]{5,4,...) while((s32[]{:T(128)}, ...), condition=%wide.region_3.4_spmd.clone.clone, body=%wide.region_2.3_spmd.clone.clone.sunk | while | flops 260067584 | bytes 8477726 | solution.py:165
  740.2 9.0 collective-permute-start.6
  770.2 7.5 collective-permute-start.6
  798.9 7.5 collective-permute-start.6
  827.5 7.5 collective-permute-start.6
  856.1 7.5 collective-permute-start.6
  884.8 7.5 collective-permute-start.6
  913.4 7.5 collective-permute-start.6
  942.0 7.5 collective-permute-start.6
  970.7 7.5 collective-permute-start.6
  999.3 7.5 collective-permute-start.6
  1027.9 7.5 collective-permute-start.6
  1056.6 7.5 collective-permute-start.6
  1085.2 7.5 collective-permute-start.6
  1113.8 7.5 collective-permute-start.6
  1142.5 7.5 collective-permute-start.6
  1171.1 7.5 collective-permute-start.6
  (1481 shorter events, 827.4 us)
Async XLA Ops:
  0.8 24.5 %collective-permute-start.11 = (f32[1,1,5,4,4,128]{5,4,3,2,1,0:T(4,128)S(1)}, f32[1,1,5,4,4,128]{5,4,3,2,1,0:T(4,128)S(1)}, u32[]{:S(2)}, u32[]{:S(2)}) collective-permute-start(f32[1,1,5,4,4,128]{5,4,3,2,1,0:T(4,128)S(1)} %get-tuple-element.788), channel_id=1, source_target_pairs={{4,0},{8,4},{12,8},{16,12},{20,16},{24,20},{28,24},{5,1},{9,5},{13... | collective-permute-start | bytes 122888 | tf_op jit(solution)/shard_map/ppermute | solution.py:26
  4.2 21.2 %collective-permute-start.12 = (f32[1,1,5,4,4,128]{5,4,3,2,1,0:T(4,128)S(1)}, f32[1,1,5,4,4,128]{5,4,3,2,1,0:T(4,128)S(1)}, u32[]{:S(2)}, u32[]{:S(2)}) collective-permute-start(f32[1,1,5,4,4,128]{5,4,3,2,1,0:T(4,128)S(1)} %get-tuple-element.785), channel_id=1, source_target_pairs={{0,1},{1,2},{2,3},{4,5},{5,6},{6,7},{8,9},{9,10},{10,11},{12,13},{... | collective-permute-start | bytes 122888 | tf_op jit(solution)/shard_map/ppermute | solution.py:26
  7.3 18.1 %collective-permute-start.13 = (f32[1,1,5,4,4,128]{5,4,3,2,1,0:T(4,128)S(1)}, f32[1,1,5,4,4,128]{5,4,3,2,1,0:T(4,128)S(1)}, u32[]{:S(2)}, u32[]{:S(2)}) collective-permute-start(f32[1,1,5,4,4,128]{5,4,3,2,1,0:T(4,128)S(1)} %get-tuple-element.786), channel_id=1, source_target_pairs={{1,0},{2,1},{3,2},{5,4},{6,5},{7,6},{9,8},{10,9},{11,10},{13,12},{... | collective-permute-start | bytes 122888 | tf_op jit(solution)/shard_map/ppermute | solution.py:26
  89.7 21.9 %collective-permute-start.26 = (f32[1,1,5,4,4,128]{5,4,3,2,1,0:T(4,128)S(1)}, f32[1,1,5,4,4,128]{5,4,3,2,1,0:T(4,128)S(1)}, u32[]{:S(2)}, u32[]{:S(2)}) collective-permute-start(f32[1,1,5,4,4,128]{5,4,3,2,1,0:T(4,128)S(1)} %get-tuple-element.757), channel_id=1, source_target_pairs={{0,4},{4,8},{8,12},{12,16},{16,20},{20,24},{24,28},{1,5},{5,9},{9,... | collective-permute-start | bytes 122888 | tf_op jit(solution)/shard_map/ppermute | solution.py:26
  100.6 17.2 %collective-permute-start.28 = (f32[1,1,5,4,4,128]{5,4,3,2,1,0:T(4,128)S(1)}, f32[1,1,5,4,4,128]{5,4,3,2,1,0:T(4,128)S(1)}, u32[]{:S(2)}, u32[]{:S(2)}) collective-permute-start(f32[1,1,5,4,4,128]{5,4,3,2,1,0:T(4,128)S(1)} %get-tuple-element.755), channel_id=1, source_target_pairs={{0,1},{1,2},{2,3},{4,5},{5,6},{6,7},{8,9},{9,10},{10,11},{12,13},{... | collective-permute-start | bytes 122888 | tf_op jit(solution)/shard_map/ppermute | solution.py:26
  103.7 26.1 %collective-permute-start.34 = (f32[1,1,5,4,4,128]{5,4,3,2,1,0:T(4,128)S(1)}, f32[1,1,5,4,4,128]{5,4,3,2,1,0:T(4,128)S(1)}, u32[]{:S(2)}, u32[]{:S(2)}) collective-permute-start(f32[1,1,5,4,4,128]{5,4,3,2,1,0:T(4,128)S(1)} %get-tuple-element.769), channel_id=1, source_target_pairs={{0,4},{4,8},{8,12},{12,16},{16,20},{20,24},{24,28},{1,5},{5,9},{9,... | collective-permute-start | bytes 122888 | tf_op jit(solution)/shard_map/ppermute | solution.py:26
  111.6 20.2 %collective-permute-start.35 = (f32[1,1,5,4,4,128]{5,4,3,2,1,0:T(4,128)S(1)}, f32[1,1,5,4,4,128]{5,4,3,2,1,0:T(4,128)S(1)}, u32[]{:S(2)}, u32[]{:S(2)}) collective-permute-start(f32[1,1,5,4,4,128]{5,4,3,2,1,0:T(4,128)S(1)} %get-tuple-element.770), channel_id=1, source_target_pairs={{4,0},{8,4},{12,8},{16,12},{20,16},{24,20},{28,24},{5,1},{9,5},{13... | collective-permute-start | bytes 122888 | tf_op jit(solution)/shard_map/ppermute | solution.py:26
  113.5 22.5 %collective-permute-start.36 = (f32[1,1,5,4,4,128]{5,4,3,2,1,0:T(4,128)S(1)}, f32[1,1,5,4,4,128]{5,4,3,2,1,0:T(4,128)S(1)}, u32[]{:S(2)}, u32[]{:S(2)}) collective-permute-start(f32[1,1,5,4,4,128]{5,4,3,2,1,0:T(4,128)S(1)} %get-tuple-element.767), channel_id=1, source_target_pairs={{0,1},{1,2},{2,3},{4,5},{5,6},{6,7},{8,9},{9,10},{10,11},{12,13},{... | collective-permute-start | bytes 122888 | tf_op jit(solution)/shard_map/ppermute | solution.py:26
  117.8 19.8 %collective-permute-start.37 = (f32[1,1,5,4,4,128]{5,4,3,2,1,0:T(4,128)S(1)}, f32[1,1,5,4,4,128]{5,4,3,2,1,0:T(4,128)S(1)}, u32[]{:S(2)}, u32[]{:S(2)}) collective-permute-start(f32[1,1,5,4,4,128]{5,4,3,2,1,0:T(4,128)S(1)} %get-tuple-element.768), channel_id=1, source_target_pairs={{1,0},{2,1},{3,2},{5,4},{6,5},{7,6},{9,8},{10,9},{11,10},{13,12},{... | collective-permute-start | bytes 122888 | tf_op jit(solution)/shard_map/ppermute | solution.py:26
  143.3 18.5 %collective-permute-start = (f32[1,1,5,4,4,128]{5,4,3,2,1,0:T(4,128)S(1)}, f32[1,1,5,4,4,128]{5,4,3,2,1,0:T(4,128)S(1)}, u32[]{:S(2)}, u32[]{:S(2)}) collective-permute-start(f32[1,1,5,4,4,128]{5,4,3,2,1,0:T(4,128)S(1)} %get-tuple-element.1030), channel_id=1, source_target_pairs={{4,0},{8,4},{12,8},{16,12},{20,16},{24,20},{28,24},{5,1},{9,5},{13... | collective-permute-start | bytes 122888 | tf_op jit(solution)/shard_map/while/body/eval_jaxpr/ppermute | solution.py:26
  173.4 17.1 %collective-permute-start = (f32[1,1,5,4,4,128]{5,4,3,2,1,0:T(4,128)S(1)}, f32[1,1,5,4,4,128]{5,4,3,2,1,0:T(4,128)S(1)}, u32[]{:S(2)}, u32[]{:S(2)}) collective-permute-start(f32[1,1,5,4,4,128]{5,4,3,2,1,0:T(4,128)S(1)} %get-tuple-element.1030), channel_id=1, source_target_pairs={{4,0},{8,4},{12,8},{16,12},{20,16},{24,20},{28,24},{5,1},{9,5},{13... | collective-permute-start | bytes 122888 | tf_op jit(solution)/shard_map/while/body/eval_jaxpr/ppermute | solution.py:26
  202.0 17.1 %collective-permute-start = (f32[1,1,5,4,4,128]{5,4,3,2,1,0:T(4,128)S(1)}, f32[1,1,5,4,4,128]{5,4,3,2,1,0:T(4,128)S(1)}, u32[]{:S(2)}, u32[]{:S(2)}) collective-permute-start(f32[1,1,5,4,4,128]{5,4,3,2,1,0:T(4,128)S(1)} %get-tuple-element.1030), channel_id=1, source_target_pairs={{4,0},{8,4},{12,8},{16,12},{20,16},{24,20},{28,24},{5,1},{9,5},{13... | collective-permute-start | bytes 122888 | tf_op jit(solution)/shard_map/while/body/eval_jaxpr/ppermute | solution.py:26
  230.7 17.1 %collective-permute-start = (f32[1,1,5,4,4,128]{5,4,3,2,1,0:T(4,128)S(1)}, f32[1,1,5,4,4,128]{5,4,3,2,1,0:T(4,128)S(1)}, u32[]{:S(2)}, u32[]{:S(2)}) collective-permute-start(f32[1,1,5,4,4,128]{5,4,3,2,1,0:T(4,128)S(1)} %get-tuple-element.1030), channel_id=1, source_target_pairs={{4,0},{8,4},{12,8},{16,12},{20,16},{24,20},{28,24},{5,1},{9,5},{13... | collective-permute-start | bytes 122888 | tf_op jit(solution)/shard_map/while/body/eval_jaxpr/ppermute | solution.py:26
  259.7 17.1 %collective-permute-start = (f32[1,1,5,4,4,128]{5,4,3,2,1,0:T(4,128)S(1)}, f32[1,1,5,4,4,128]{5,4,3,2,1,0:T(4,128)S(1)}, u32[]{:S(2)}, u32[]{:S(2)}) collective-permute-start(f32[1,1,5,4,4,128]{5,4,3,2,1,0:T(4,128)S(1)} %get-tuple-element.1030), channel_id=1, source_target_pairs={{4,0},{8,4},{12,8},{16,12},{20,16},{24,20},{28,24},{5,1},{9,5},{13... | collective-permute-start | bytes 122888 | tf_op jit(solution)/shard_map/while/body/eval_jaxpr/ppermute | solution.py:26
  288.4 17.1 %collective-permute-start = (f32[1,1,5,4,4,128]{5,4,3,2,1,0:T(4,128)S(1)}, f32[1,1,5,4,4,128]{5,4,3,2,1,0:T(4,128)S(1)}, u32[]{:S(2)}, u32[]{:S(2)}) collective-permute-start(f32[1,1,5,4,4,128]{5,4,3,2,1,0:T(4,128)S(1)} %get-tuple-element.1030), channel_id=1, source_target_pairs={{4,0},{8,4},{12,8},{16,12},{20,16},{24,20},{28,24},{5,1},{9,5},{13... | collective-permute-start | bytes 122888 | tf_op jit(solution)/shard_map/while/body/eval_jaxpr/ppermute | solution.py:26
  317.0 17.1 %collective-permute-start = (f32[1,1,5,4,4,128]{5,4,3,2,1,0:T(4,128)S(1)}, f32[1,1,5,4,4,128]{5,4,3,2,1,0:T(4,128)S(1)}, u32[]{:S(2)}, u32[]{:S(2)}) collective-permute-start(f32[1,1,5,4,4,128]{5,4,3,2,1,0:T(4,128)S(1)} %get-tuple-element.1030), channel_id=1, source_target_pairs={{4,0},{8,4},{12,8},{16,12},{20,16},{24,20},{28,24},{5,1},{9,5},{13... | collective-permute-start | bytes 122888 | tf_op jit(solution)/shard_map/while/body/eval_jaxpr/ppermute | solution.py:26
  345.6 17.1 %collective-permute-start = (f32[1,1,5,4,4,128]{5,4,3,2,1,0:T(4,128)S(1)}, f32[1,1,5,4,4,128]{5,4,3,2,1,0:T(4,128)S(1)}, u32[]{:S(2)}, u32[]{:S(2)}) collective-permute-start(f32[1,1,5,4,4,128]{5,4,3,2,1,0:T(4,128)S(1)} %get-tuple-element.1030), channel_id=1, source_target_pairs={{4,0},{8,4},{12,8},{16,12},{20,16},{24,20},{28,24},{5,1},{9,5},{13... | collective-permute-start | bytes 122888 | tf_op jit(solution)/shard_map/while/body/eval_jaxpr/ppermute | solution.py:26
  374.2 17.1 %collective-permute-start = (f32[1,1,5,4,4,128]{5,4,3,2,1,0:T(4,128)S(1)}, f32[1,1,5,4,4,128]{5,4,3,2,1,0:T(4,128)S(1)}, u32[]{:S(2)}, u32[]{:S(2)}) collective-permute-start(f32[1,1,5,4,4,128]{5,4,3,2,1,0:T(4,128)S(1)} %get-tuple-element.1030), channel_id=1, source_target_pairs={{4,0},{8,4},{12,8},{16,12},{20,16},{24,20},{28,24},{5,1},{9,5},{13... | collective-permute-start | bytes 122888 | tf_op jit(solution)/shard_map/while/body/eval_jaxpr/ppermute | solution.py:26
  402.8 17.1 %collective-permute-start = (f32[1,1,5,4,4,128]{5,4,3,2,1,0:T(4,128)S(1)}, f32[1,1,5,4,4,128]{5,4,3,2,1,0:T(4,128)S(1)}, u32[]{:S(2)}, u32[]{:S(2)}) collective-permute-start(f32[1,1,5,4,4,128]{5,4,3,2,1,0:T(4,128)S(1)} %get-tuple-element.1030), channel_id=1, source_target_pairs={{4,0},{8,4},{12,8},{16,12},{20,16},{24,20},{28,24},{5,1},{9,5},{13... | collective-permute-start | bytes 122888 | tf_op jit(solution)/shard_map/while/body/eval_jaxpr/ppermute | solution.py:26
  431.5 17.1 %collective-permute-start = (f32[1,1,5,4,4,128]{5,4,3,2,1,0:T(4,128)S(1)}, f32[1,1,5,4,4,128]{5,4,3,2,1,0:T(4,128)S(1)}, u32[]{:S(2)}, u32[]{:S(2)}) collective-permute-start(f32[1,1,5,4,4,128]{5,4,3,2,1,0:T(4,128)S(1)} %get-tuple-element.1030), channel_id=1, source_target_pairs={{4,0},{8,4},{12,8},{16,12},{20,16},{24,20},{28,24},{5,1},{9,5},{13... | collective-permute-start | bytes 122888 | tf_op jit(solution)/shard_map/while/body/eval_jaxpr/ppermute | solution.py:26
  460.1 17.1 %collective-permute-start = (f32[1,1,5,4,4,128]{5,4,3,2,1,0:T(4,128)S(1)}, f32[1,1,5,4,4,128]{5,4,3,2,1,0:T(4,128)S(1)}, u32[]{:S(2)}, u32[]{:S(2)}) collective-permute-start(f32[1,1,5,4,4,128]{5,4,3,2,1,0:T(4,128)S(1)} %get-tuple-element.1030), channel_id=1, source_target_pairs={{4,0},{8,4},{12,8},{16,12},{20,16},{24,20},{28,24},{5,1},{9,5},{13... | collective-permute-start | bytes 122888 | tf_op jit(solution)/shard_map/while/body/eval_jaxpr/ppermute | solution.py:26
  488.7 17.1 %collective-permute-start = (f32[1,1,5,4,4,128]{5,4,3,2,1,0:T(4,128)S(1)}, f32[1,1,5,4,4,128]{5,4,3,2,1,0:T(4,128)S(1)}, u32[]{:S(2)}, u32[]{:S(2)}) collective-permute-start(f32[1,1,5,4,4,128]{5,4,3,2,1,0:T(4,128)S(1)} %get-tuple-element.1030), channel_id=1, source_target_pairs={{4,0},{8,4},{12,8},{16,12},{20,16},{24,20},{28,24},{5,1},{9,5},{13... | collective-permute-start | bytes 122888 | tf_op jit(solution)/shard_map/while/body/eval_jaxpr/ppermute | solution.py:26
  517.3 17.1 %collective-permute-start = (f32[1,1,5,4,4,128]{5,4,3,2,1,0:T(4,128)S(1)}, f32[1,1,5,4,4,128]{5,4,3,2,1,0:T(4,128)S(1)}, u32[]{:S(2)}, u32[]{:S(2)}) collective-permute-start(f32[1,1,5,4,4,128]{5,4,3,2,1,0:T(4,128)S(1)} %get-tuple-element.1030), channel_id=1, source_target_pairs={{4,0},{8,4},{12,8},{16,12},{20,16},{24,20},{28,24},{5,1},{9,5},{13... | collective-permute-start | bytes 122888 | tf_op jit(solution)/shard_map/while/body/eval_jaxpr/ppermute | solution.py:26
  546.0 17.1 %collective-permute-start = (f32[1,1,5,4,4,128]{5,4,3,2,1,0:T(4,128)S(1)}, f32[1,1,5,4,4,128]{5,4,3,2,1,0:T(4,128)S(1)}, u32[]{:S(2)}, u32[]{:S(2)}) collective-permute-start(f32[1,1,5,4,4,128]{5,4,3,2,1,0:T(4,128)S(1)} %get-tuple-element.1030), channel_id=1, source_target_pairs={{4,0},{8,4},{12,8},{16,12},{20,16},{24,20},{28,24},{5,1},{9,5},{13... | collective-permute-start | bytes 122888 | tf_op jit(solution)/shard_map/while/body/eval_jaxpr/ppermute | solution.py:26
  574.6 17.1 %collective-permute-start = (f32[1,1,5,4,4,128]{5,4,3,2,1,0:T(4,128)S(1)}, f32[1,1,5,4,4,128]{5,4,3,2,1,0:T(4,128)S(1)}, u32[]{:S(2)}, u32[]{:S(2)}) collective-permute-start(f32[1,1,5,4,4,128]{5,4,3,2,1,0:T(4,128)S(1)} %get-tuple-element.1030), channel_id=1, source_target_pairs={{4,0},{8,4},{12,8},{16,12},{20,16},{24,20},{28,24},{5,1},{9,5},{13... | collective-permute-start | bytes 122888 | tf_op jit(solution)/shard_map/while/body/eval_jaxpr/ppermute | solution.py:26
  685.3 21.0 %collective-permute-start.54 = (f32[1,1,5,4,4,128]{5,4,3,2,1,0:T(4,128)S(1)}, f32[1,1,5,4,4,128]{5,4,3,2,1,0:T(4,128)S(1)}, u32[]{:S(2)}, u32[]{:S(2)}) collective-permute-start(f32[1,1,5,4,4,128]{5,4,3,2,1,0:T(4,128)S(1)} %get-tuple-element.727), channel_id=1, source_target_pairs={{0,4},{4,8},{8,12},{12,16},{16,20},{20,24},{24,28},{1,5},{5,9},{9,... | collective-permute-start | bytes 122888 | tf_op jit(solution)/shard_map/ppermute | solution.py:26
  695.3 17.2 %collective-permute-start.56 = (f32[1,1,5,4,4,128]{5,4,3,2,1,0:T(4,128)S(1)}, f32[1,1,5,4,4,128]{5,4,3,2,1,0:T(4,128)S(1)}, u32[]{:S(2)}, u32[]{:S(2)}) collective-permute-start(f32[1,1,5,4,4,128]{5,4,3,2,1,0:T(4,128)S(1)} %get-tuple-element.725), channel_id=1, source_target_pairs={{0,1},{1,2},{2,3},{4,5},{5,6},{6,7},{8,9},{9,10},{10,11},{12,13},{... | collective-permute-start | bytes 122888 | tf_op jit(solution)/shard_map/ppermute | solution.py:26
  697.0 17.0 %collective-permute-start.57 = (f32[1,1,5,4,4,128]{5,4,3,2,1,0:T(4,128)S(1)}, f32[1,1,5,4,4,128]{5,4,3,2,1,0:T(4,128)S(1)}, u32[]{:S(2)}, u32[]{:S(2)}) collective-permute-start(f32[1,1,5,4,4,128]{5,4,3,2,1,0:T(4,128)S(1)} %get-tuple-element.726), channel_id=1, source_target_pairs={{1,0},{2,1},{3,2},{5,4},{6,5},{7,6},{9,8},{10,9},{11,10},{13,12},{... | collective-permute-start | bytes 122888 | tf_op jit(solution)/shard_map/ppermute | solution.py:26
  698.5 26.2 %collective-permute-start.62 = (f32[1,1,5,4,4,128]{5,4,3,2,1,0:T(4,128)S(1)}, f32[1,1,5,4,4,128]{5,4,3,2,1,0:T(4,128)S(1)}, u32[]{:S(2)}, u32[]{:S(2)}) collective-permute-start(f32[1,1,5,4,4,128]{5,4,3,2,1,0:T(4,128)S(1)} %get-tuple-element.721), channel_id=1, source_target_pairs={{0,4},{4,8},{8,12},{12,16},{16,20},{20,24},{24,28},{1,5},{5,9},{9,... | collective-permute-start | bytes 122888 | tf_op jit(solution)/shard_map/ppermute | solution.py:26
  706.3 20.3 %collective-permute-start.63 = (f32[1,1,5,4,4,128]{5,4,3,2,1,0:T(4,128)S(1)}, f32[1,1,5,4,4,128]{5,4,3,2,1,0:T(4,128)S(1)}, u32[]{:S(2)}, u32[]{:S(2)}) collective-permute-start(f32[1,1,5,4,4,128]{5,4,3,2,1,0:T(4,128)S(1)} %get-tuple-element.722), channel_id=1, source_target_pairs={{4,0},{8,4},{12,8},{16,12},{20,16},{24,20},{28,24},{5,1},{9,5},{13... | collective-permute-start | bytes 122888 | tf_op jit(solution)/shard_map/ppermute | solution.py:26
  708.3 22.7 %collective-permute-start.64 = (f32[1,1,5,4,4,128]{5,4,3,2,1,0:T(4,128)S(1)}, f32[1,1,5,4,4,128]{5,4,3,2,1,0:T(4,128)S(1)}, u32[]{:S(2)}, u32[]{:S(2)}) collective-permute-start(f32[1,1,5,4,4,128]{5,4,3,2,1,0:T(4,128)S(1)} %get-tuple-element.719), channel_id=1, source_target_pairs={{0,1},{1,2},{2,3},{4,5},{5,6},{6,7},{8,9},{9,10},{10,11},{12,13},{... | collective-permute-start | bytes 122888 | tf_op jit(solution)/shard_map/ppermute | solution.py:26
  712.6 19.8 %collective-permute-start.65 = (f32[1,1,5,4,4,128]{5,4,3,2,1,0:T(4,128)S(1)}, f32[1,1,5,4,4,128]{5,4,3,2,1,0:T(4,128)S(1)}, u32[]{:S(2)}, u32[]{:S(2)}) collective-permute-start(f32[1,1,5,4,4,128]{5,4,3,2,1,0:T(4,128)S(1)} %get-tuple-element.720), channel_id=1, source_target_pairs={{1,0},{2,1},{3,2},{5,4},{6,5},{7,6},{9,8},{10,9},{11,10},{13,12},{... | collective-permute-start | bytes 122888 | tf_op jit(solution)/shard_map/ppermute | solution.py:26
  738.3 18.5 %collective-permute-start.5 = (f32[1,1,5,4,4,128]{5,4,3,2,1,0:T(4,128)S(1)}, f32[1,1,5,4,4,128]{5,4,3,2,1,0:T(4,128)S(1)}, u32[]{:S(2)}, u32[]{:S(2)}) collective-permute-start(f32[1,1,5,4,4,128]{5,4,3,2,1,0:T(4,128)S(1)} %get-tuple-element.1054), channel_id=1, source_target_pairs={{4,0},{8,4},{12,8},{16,12},{20,16},{24,20},{28,24},{5,1},{9,5},{13... | collective-permute-start | bytes 122888 | tf_op jit(solution)/shard_map/while/body/eval_jaxpr/ppermute | solution.py:26
  768.3 17.1 %collective-permute-start.5 = (f32[1,1,5,4,4,128]{5,4,3,2,1,0:T(4,128)S(1)}, f32[1,1,5,4,4,128]{5,4,3,2,1,0:T(4,128)S(1)}, u32[]{:S(2)}, u32[]{:S(2)}) collective-permute-start(f32[1,1,5,4,4,128]{5,4,3,2,1,0:T(4,128)S(1)} %get-tuple-element.1054), channel_id=1, source_target_pairs={{4,0},{8,4},{12,8},{16,12},{20,16},{24,20},{28,24},{5,1},{9,5},{13... | collective-permute-start | bytes 122888 | tf_op jit(solution)/shard_map/while/body/eval_jaxpr/ppermute | solution.py:26
  796.9 17.1 %collective-permute-start.5 = (f32[1,1,5,4,4,128]{5,4,3,2,1,0:T(4,128)S(1)}, f32[1,1,5,4,4,128]{5,4,3,2,1,0:T(4,128)S(1)}, u32[]{:S(2)}, u32[]{:S(2)}) collective-permute-start(f32[1,1,5,4,4,128]{5,4,3,2,1,0:T(4,128)S(1)} %get-tuple-element.1054), channel_id=1, source_target_pairs={{4,0},{8,4},{12,8},{16,12},{20,16},{24,20},{28,24},{5,1},{9,5},{13... | collective-permute-start | bytes 122888 | tf_op jit(solution)/shard_map/while/body/eval_jaxpr/ppermute | solution.py:26
  825.6 17.1 %collective-permute-start.5 = (f32[1,1,5,4,4,128]{5,4,3,2,1,0:T(4,128)S(1)}, f32[1,1,5,4,4,128]{5,4,3,2,1,0:T(4,128)S(1)}, u32[]{:S(2)}, u32[]{:S(2)}) collective-permute-start(f32[1,1,5,4,4,128]{5,4,3,2,1,0:T(4,128)S(1)} %get-tuple-element.1054), channel_id=1, source_target_pairs={{4,0},{8,4},{12,8},{16,12},{20,16},{24,20},{28,24},{5,1},{9,5},{13... | collective-permute-start | bytes 122888 | tf_op jit(solution)/shard_map/while/body/eval_jaxpr/ppermute | solution.py:26
  854.2 17.1 %collective-permute-start.5 = (f32[1,1,5,4,4,128]{5,4,3,2,1,0:T(4,128)S(1)}, f32[1,1,5,4,4,128]{5,4,3,2,1,0:T(4,128)S(1)}, u32[]{:S(2)}, u32[]{:S(2)}) collective-permute-start(f32[1,1,5,4,4,128]{5,4,3,2,1,0:T(4,128)S(1)} %get-tuple-element.1054), channel_id=1, source_target_pairs={{4,0},{8,4},{12,8},{16,12},{20,16},{24,20},{28,24},{5,1},{9,5},{13... | collective-permute-start | bytes 122888 | tf_op jit(solution)/shard_map/while/body/eval_jaxpr/ppermute | solution.py:26
  882.8 17.1 %collective-permute-start.5 = (f32[1,1,5,4,4,128]{5,4,3,2,1,0:T(4,128)S(1)}, f32[1,1,5,4,4,128]{5,4,3,2,1,0:T(4,128)S(1)}, u32[]{:S(2)}, u32[]{:S(2)}) collective-permute-start(f32[1,1,5,4,4,128]{5,4,3,2,1,0:T(4,128)S(1)} %get-tuple-element.1054), channel_id=1, source_target_pairs={{4,0},{8,4},{12,8},{16,12},{20,16},{24,20},{28,24},{5,1},{9,5},{13... | collective-permute-start | bytes 122888 | tf_op jit(solution)/shard_map/while/body/eval_jaxpr/ppermute | solution.py:26
  911.5 17.1 %collective-permute-start.5 = (f32[1,1,5,4,4,128]{5,4,3,2,1,0:T(4,128)S(1)}, f32[1,1,5,4,4,128]{5,4,3,2,1,0:T(4,128)S(1)}, u32[]{:S(2)}, u32[]{:S(2)}) collective-permute-start(f32[1,1,5,4,4,128]{5,4,3,2,1,0:T(4,128)S(1)} %get-tuple-element.1054), channel_id=1, source_target_pairs={{4,0},{8,4},{12,8},{16,12},{20,16},{24,20},{28,24},{5,1},{9,5},{13... | collective-permute-start | bytes 122888 | tf_op jit(solution)/shard_map/while/body/eval_jaxpr/ppermute | solution.py:26
  940.1 17.1 %collective-permute-start.5 = (f32[1,1,5,4,4,128]{5,4,3,2,1,0:T(4,128)S(1)}, f32[1,1,5,4,4,128]{5,4,3,2,1,0:T(4,128)S(1)}, u32[]{:S(2)}, u32[]{:S(2)}) collective-permute-start(f32[1,1,5,4,4,128]{5,4,3,2,1,0:T(4,128)S(1)} %get-tuple-element.1054), channel_id=1, source_target_pairs={{4,0},{8,4},{12,8},{16,12},{20,16},{24,20},{28,24},{5,1},{9,5},{13... | collective-permute-start | bytes 122888 | tf_op jit(solution)/shard_map/while/body/eval_jaxpr/ppermute | solution.py:26
  968.7 17.1 %collective-permute-start.5 = (f32[1,1,5,4,4,128]{5,4,3,2,1,0:T(4,128)S(1)}, f32[1,1,5,4,4,128]{5,4,3,2,1,0:T(4,128)S(1)}, u32[]{:S(2)}, u32[]{:S(2)}) collective-permute-start(f32[1,1,5,4,4,128]{5,4,3,2,1,0:T(4,128)S(1)} %get-tuple-element.1054), channel_id=1, source_target_pairs={{4,0},{8,4},{12,8},{16,12},{20,16},{24,20},{28,24},{5,1},{9,5},{13... | collective-permute-start | bytes 122888 | tf_op jit(solution)/shard_map/while/body/eval_jaxpr/ppermute | solution.py:26
  997.4 17.1 %collective-permute-start.5 = (f32[1,1,5,4,4,128]{5,4,3,2,1,0:T(4,128)S(1)}, f32[1,1,5,4,4,128]{5,4,3,2,1,0:T(4,128)S(1)}, u32[]{:S(2)}, u32[]{:S(2)}) collective-permute-start(f32[1,1,5,4,4,128]{5,4,3,2,1,0:T(4,128)S(1)} %get-tuple-element.1054), channel_id=1, source_target_pairs={{4,0},{8,4},{12,8},{16,12},{20,16},{24,20},{28,24},{5,1},{9,5},{13... | collective-permute-start | bytes 122888 | tf_op jit(solution)/shard_map/while/body/eval_jaxpr/ppermute | solution.py:26
  1026.0 17.1 %collective-permute-start.5 = (f32[1,1,5,4,4,128]{5,4,3,2,1,0:T(4,128)S(1)}, f32[1,1,5,4,4,128]{5,4,3,2,1,0:T(4,128)S(1)}, u32[]{:S(2)}, u32[]{:S(2)}) collective-permute-start(f32[1,1,5,4,4,128]{5,4,3,2,1,0:T(4,128)S(1)} %get-tuple-element.1054), channel_id=1, source_target_pairs={{4,0},{8,4},{12,8},{16,12},{20,16},{24,20},{28,24},{5,1},{9,5},{13... | collective-permute-start | bytes 122888 | tf_op jit(solution)/shard_map/while/body/eval_jaxpr/ppermute | solution.py:26
  1054.6 17.1 %collective-permute-start.5 = (f32[1,1,5,4,4,128]{5,4,3,2,1,0:T(4,128)S(1)}, f32[1,1,5,4,4,128]{5,4,3,2,1,0:T(4,128)S(1)}, u32[]{:S(2)}, u32[]{:S(2)}) collective-permute-start(f32[1,1,5,4,4,128]{5,4,3,2,1,0:T(4,128)S(1)} %get-tuple-element.1054), channel_id=1, source_target_pairs={{4,0},{8,4},{12,8},{16,12},{20,16},{24,20},{28,24},{5,1},{9,5},{13... | collective-permute-start | bytes 122888 | tf_op jit(solution)/shard_map/while/body/eval_jaxpr/ppermute | solution.py:26
  1083.3 17.1 %collective-permute-start.5 = (f32[1,1,5,4,4,128]{5,4,3,2,1,0:T(4,128)S(1)}, f32[1,1,5,4,4,128]{5,4,3,2,1,0:T(4,128)S(1)}, u32[]{:S(2)}, u32[]{:S(2)}) collective-permute-start(f32[1,1,5,4,4,128]{5,4,3,2,1,0:T(4,128)S(1)} %get-tuple-element.1054), channel_id=1, source_target_pairs={{4,0},{8,4},{12,8},{16,12},{20,16},{24,20},{28,24},{5,1},{9,5},{13... | collective-permute-start | bytes 122888 | tf_op jit(solution)/shard_map/while/body/eval_jaxpr/ppermute | solution.py:26
  1111.9 17.1 %collective-permute-start.5 = (f32[1,1,5,4,4,128]{5,4,3,2,1,0:T(4,128)S(1)}, f32[1,1,5,4,4,128]{5,4,3,2,1,0:T(4,128)S(1)}, u32[]{:S(2)}, u32[]{:S(2)}) collective-permute-start(f32[1,1,5,4,4,128]{5,4,3,2,1,0:T(4,128)S(1)} %get-tuple-element.1054), channel_id=1, source_target_pairs={{4,0},{8,4},{12,8},{16,12},{20,16},{24,20},{28,24},{5,1},{9,5},{13... | collective-permute-start | bytes 122888 | tf_op jit(solution)/shard_map/while/body/eval_jaxpr/ppermute | solution.py:26
  1140.5 17.1 %collective-permute-start.5 = (f32[1,1,5,4,4,128]{5,4,3,2,1,0:T(4,128)S(1)}, f32[1,1,5,4,4,128]{5,4,3,2,1,0:T(4,128)S(1)}, u32[]{:S(2)}, u32[]{:S(2)}) collective-permute-start(f32[1,1,5,4,4,128]{5,4,3,2,1,0:T(4,128)S(1)} %get-tuple-element.1054), channel_id=1, source_target_pairs={{4,0},{8,4},{12,8},{16,12},{20,16},{24,20},{28,24},{5,1},{9,5},{13... | collective-permute-start | bytes 122888 | tf_op jit(solution)/shard_map/while/body/eval_jaxpr/ppermute | solution.py:26
  1169.2 17.1 %collective-permute-start.5 = (f32[1,1,5,4,4,128]{5,4,3,2,1,0:T(4,128)S(1)}, f32[1,1,5,4,4,128]{5,4,3,2,1,0:T(4,128)S(1)}, u32[]{:S(2)}, u32[]{:S(2)}) collective-permute-start(f32[1,1,5,4,4,128]{5,4,3,2,1,0:T(4,128)S(1)} %get-tuple-element.1054), channel_id=1, source_target_pairs={{4,0},{8,4},{12,8},{16,12},{20,16},{24,20},{28,24},{5,1},{9,5},{13... | collective-permute-start | bytes 122888 | tf_op jit(solution)/shard_map/while/body/eval_jaxpr/ppermute | solution.py:26
  (204 other events, 1890.7 us)
where the time goes:
time: 1210 us; the launch traced here: 1200 us
  starting transfers between devices  736 us (61%)
  waiting for transfers between devices  245 us (20%)
  matrix products  135 us (11%)
  local copies, waits for them, and re-layouts  47.7 us (4%)
  other arithmetic  24.4 us (2%)
    ppermute x216, starting transfers between devices, passed_along(): return lax.ppermute(block, axis, route)  736 us
    ppermute x216, waiting for transfers between devices, passed_along(): return lax.ppermute(block, axis, route)  245 us
    dot_general x46, matrix products, apply_operator(): jnp.einsum('dgf,dbxyfmz->bxygmz', flux_jacobian, slopes, precision=HIGHEST)  45.3 us
    dot_general x46, matrix products, apply_operator(): slopes = jnp.einsum('dmn,bxyfnz->dbxyfmz', grads, field, precision=HIGHEST)  26.4 us
    dot_general x76, matrix products, precondition(): jnp.einsum('kn,bxyfkz->bxyfnz', basis, modes * inverse, precision=HIGHEST)  26 us
  transfers between devices with their start and end apart: 216, of which 47 were waited for; matrix products, arithmetic and copies ran while one was open for 8% of the time, Pallas kernels for 0%

commit v1 on v0

v1 whole, which is shorter than its diff:
```python
import functools
import math

import jax
import jax.numpy as jnp
import ml_dtypes
import numpy as np
from jax import lax
from jax.experimental import pallas as pl
from jax.experimental.pallas import tpu as pltpu
from jax.sharding import PartitionSpec as P

FIELDS, NODES, EZ = 5, 64, 128
WIDE = FIELDS * EZ
NT, NX, NY = 16, 8, 4
DT = 0.1
H1 = 0.05
H2 = 0.1
MESH = pl.DeviceIdType.MESH
F32 = jnp.float32
BF16 = jnp.bfloat16


def tables():
    eye = np.eye(4)
    k = np.arange(4)
    cosine = np.where(k == 0, 0.5, math.sqrt(0.5))[:, None] * np.cos(math.pi * k[:, None] * (2 * k[None, :] + 1) / 8)
    grad = 0.5 * np.eye(4, k=1) - 0.5 * np.eye(4, k=-1)
    slope = cosine @ grad @ cosine.T
    eigen = 2 - 2 * np.cos(math.pi * k / 4)
    spectrum = (eigen[:, None, None] + eigen[None, :, None] + eigen[None, None, :]).reshape(64) + 3.0

    def kron3(a, b, c):
        return np.kron(np.kron(a, b), c)

    low, high = cosine[:, :1].T, cosine[:, 3:].T
    faces_xy = np.concatenate([kron3(low, eye, eye), kron3(high, eye, eye), kron3(eye, low, eye), kron3(eye, high, eye)])
    faces_z = np.concatenate([kron3(eye, eye, low), kron3(eye, eye, high)])
    slopes = np.concatenate([kron3(slope, eye, eye), kron3(eye, slope, eye), kron3(eye, eye, slope)])

    def parts(w):
        w = w.astype(np.float32)
        high_part = w.astype(ml_dtypes.bfloat16)
        low_part = (w - high_part.astype(np.float32)).astype(ml_dtypes.bfloat16)
        return np.concatenate([high_part, high_part, low_part], axis=1)

    basis = kron3(cosine, cosine, cosine).astype(np.float32)
    return (
        parts(faces_xy),
        parts(np.concatenate([slopes, faces_z])),
        parts(faces_xy.T),
        parts(faces_z.T),
        basis,
        np.ascontiguousarray(basis.T),
        np.repeat(spectrum.astype(np.float32)[:, None], EZ, axis=1),
    )


def worker(t, ex, ey):
    return {"tm": ex // 2 * 4 + t % 4, "sx": t // 4 * 2 + ex % 2, "sy": ey}


def wide(x):
    return jnp.concatenate([x] * FIELDS, axis=1)


def split(x):
    high = x.astype(BF16)
    low = (x - high.astype(F32)).astype(BF16)
    return jnp.concatenate([high, low, high], axis=0)


def apply(table, pieces):
    return jnp.dot(table[...], pieces, preferred_element_type=F32)


def exact(table, x):
    return jnp.dot(table[...], x, preferred_element_type=F32, precision=lax.Precision.HIGHEST)


def kernel(initial, viscosity, jac, faces_t, local_t, inject_t, inject_z, basis, basis_t, spectrum, out,
           own, inp, send, recv, st, bs, rh, got,
           in_sem, send_sem, recv_sem, b_send, b_recv, r_send, got_sem, end_send):
    tm, sx, sy = lax.axis_index("tm"), lax.axis_index("sx"), lax.axis_index("sy")
    t = sx // 2 * 4 + tm % 4
    ex = tm // 4 * 2 + sx % 2
    ey = sy
    root = t == 0
    target = {"tm": sx // 2 * 4 + tm // 4, "sx": tm % 4 * 2 + sx % 2, "sy": sy}
    source = {"tm": tm % 4 * 4 + sx // 2, "sx": tm // 4 * 2 + sx % 2, "sy": sy}
    moved = jnp.logical_not(jnp.logical_and(tm // 4 == sx // 2, tm % 4 == sx // 2))
    owner = {"tm": t, "sx": ex, "sy": ey}
    apart = tm // 4 != sx // 2
    around = [
        (worker(t, ex - 1, ey), ex > 0, 0),
        (worker(t, ex + 1, ey), ex < NX - 1, 1),
        (worker(t, ex, ey - 1), ey > 0, 2),
        (worker(t, ex, ey + 1), ey < NY - 1, 3),
    ]
    (D1, D2, CL, HC, U0, U2, M, RM, T0, E1, RU0, RU2, U1N, RU1N, O, G, K0, TMP) = range(18)

    for _, there, side in around:
        @pl.when(jnp.logical_not(there))
        def _(side=side):
            for slot in range(2):
                recv[slot, side] = jnp.zeros((32, WIDE), F32)

    barrier = pltpu.get_barrier_semaphore()

    def greet(device):
        pl.semaphore_signal(barrier, inc=1, device_id=device, device_id_type=MESH)

    for device, there, _ in around:
        @pl.when(there)
        def _(device=device):
            greet(device)

    @pl.when(moved)
    def _():
        greet(source)

    @pl.when(apart)
    def _():
        greet(owner)

    @pl.when(tm > 0)
    def _():
        greet(worker(0, sx, sy))

    @pl.when(tm < NT - 1)
    def _():
        greet({"tm": tm + 1, "sx": sx, "sy": sy})

    @pl.when(root)
    def _():
        def one(k, carry):
            greet(worker(k, ex, ey))
            return carry
        lax.fori_loop(1, NT, one, 0)

    nodal = jnp.concatenate([initial[0, 0, f] for f in range(FIELDS)], axis=1)
    own[0:NODES] = exact(basis, nodal)
    own[NODES:NODES + 8] = wide(jnp.broadcast_to(viscosity[0], (8, EZ)))

    expected = jnp.where(root, NT - 1, 1)
    for there in [there for _, there, _ in around] + [moved, apart, tm > 0]:
        expected = expected + jnp.where(there, 1, 0)
    pl.semaphore_wait(barrier, expected)

    def bring():
        return pltpu.make_async_remote_copy(src_ref=own, dst_ref=inp, send_sem=in_sem.at[0], recv_sem=in_sem.at[1],
                                            device_id=target, device_id_type=MESH)

    @pl.when(moved)
    def _():
        bring().start()
        bring().wait()

    @pl.when(jnp.logical_not(moved))
    def _():
        inp[...] = own[...]

    @pl.when(tm == 0)
    def _():
        got[0] = own[0:NODES]

    c = inp[NODES:NODES + 8, 0:EZ][0:1]
    cl = c * spectrum[...]
    st[CL] = wide(cl)
    st[D1] = wide(1.0 / (1.0 + H1 * cl))
    st[D2] = wide(1.0 / (1.0 + H2 * cl))
    st[HC] = wide(jnp.broadcast_to(0.5 * c, (NODES, EZ)))
    st[U0] = inp[0:NODES]
    st[U2] = inp[0:NODES]
    st[M] = jnp.zeros((NODES, WIDE), F32)
    st[RM] = jnp.zeros((NODES, WIDE), F32)
    lane = lax.broadcasted_iota(jnp.int32, (16, EZ), 1)

    def fields_of(x):
        return [x[:, f * EZ:(f + 1) * EZ] for f in range(FIELDS)]

    def local_part(pieces):
        made = apply(local_t, pieces)
        slopes = [fields_of(made[d * NODES:(d + 1) * NODES]) for d in range(3)]
        transport = []
        for g in range(FIELDS):
            total = None
            for d in range(3):
                for f in range(FIELDS):
                    term = jac[d, g, f] * slopes[d][f]
                    total = term if total is None else total + term
            transport.append(total)
        low = [jnp.where(lane == EZ - 1, 0.0, pltpu.roll(x, EZ - 1, 1)) for x in fields_of(made[192:208])]
        high = [jnp.where(lane == 0, 0.0, pltpu.roll(x, 1, 1)) for x in fields_of(made[208:224])]
        shifted = jnp.concatenate([jnp.concatenate(high, axis=1), jnp.concatenate(low, axis=1)], axis=0)
        return jnp.concatenate(transport, axis=1) - st[HC] * apply(inject_z, split(shifted))

    def couple(values, turn):
        slot = turn % 2
        rows = 16 * len(values)
        pieces = [split(v) for v in values]
        for i, p in enumerate(pieces):
            made = apply(faces_t, p)
            for k in range(4):
                send[k, 16 * i:16 * i + 16] = made[16 * k:16 * k + 16]

        def copy(device, k, side):
            return pltpu.make_async_remote_copy(
                src_ref=send.at[k, pl.ds(0, rows)], dst_ref=recv.at[slot, side, pl.ds(0, rows)],
                send_sem=send_sem.at[k], recv_sem=recv_sem.at[slot, side], device_id=device, device_id_type=MESH)

        for device, there, k in around:
            @pl.when(there)
            def _(device=device, k=k):
                copy(device, k, k ^ 1).start()
        results = [local_part(p) for p in pieces]
        for device, there, k in around:
            @pl.when(there)
            def _(device=device, k=k):
                copy(device, k, k).wait_recv()
        for device, there, k in around:
            @pl.when(there)
            def _(device=device, k=k):
                copy(device, k, k ^ 1).wait_send()
        for i in range(len(values)):
            came = jnp.concatenate([recv[slot, k, 16 * i:16 * i + 16] for k in range(4)], axis=0)
            results[i] = results[i] - st[HC] * apply(inject_t, split(came))
        return results

    def sweep(turn_of):
        st[RU0], st[RU2] = couple([st[U0], st[U2]], turn_of)
        u1 = st[M] + 0.5 * (st[U0] + st[U2])
        ru1 = st[RM] + 0.5 * (st[RU0] + st[RU2])
        k0 = st[CL] * st[U0] + st[RU0]
        k1 = st[CL] * u1 + ru1
        k2 = st[CL] * st[U2] + st[RU2]
        st[K0] = k0
        t0 = st[U0] + H1 * k1 - DT * (5.0 / 24.0 * k0 + 1.0 / 3.0 * k1 - 1.0 / 24.0 * k2)
        st[T0] = t0
        st[E1] = H1 * k2 - DT * (-1.0 / 24.0 * k0 + 1.0 / 3.0 * k1 + 5.0 / 24.0 * k2)
        st[TMP] = st[D1] * (t0 - H1 * ru1)

        def turn(i, carry):
            (rv,) = couple([st[TMP]], turn_of + 1 + i)
            st[TMP] = st[D1] * (st[T0] - H1 * rv)
            return carry
        lax.fori_loop(0, 2, turn, 0)
        u1n = st[TMP]
        st[U1N] = u1n
        t1 = u1n + st[E1]
        st[T0] = t1
        rw, ru1n = couple([st[D1] * (t1 - H1 * st[RU2]), u1n], turn_of + 3)
        st[RU1N] = ru1n
        (rw,) = couple([st[D1] * (st[T0] - H1 * rw)], turn_of + 4)
        u2n = st[D1] * (st[T0] - H1 * rw)
        st[TMP] = u2n
        (ru2n,) = couple([u2n], turn_of + 5)
        u2n = st[TMP]
        k1n = st[CL] * st[U1N] + st[RU1N]
        k2n = st[CL] * u2n + ru2n
        o = -DT * (1.0 / 6.0 * st[K0] + 2.0 / 3.0 * k1n - 5.0 / 6.0 * k2n)
        st[O] = o
        st[G] = st[D2] * (o - H2 * ru2n)
        st[M] = st[U1N] - 0.5 * (st[U0] + u2n)
        st[RM] = st[RU1N] - 0.5 * (st[RU0] + ru2n)

    def iteration(it, carry):
        sweep(it * (7 + t))

        @pl.when(it == 0)
        def _():
            def chain(i, carry):
                s = st[U2] * 1.0
                s = jnp.where(i == 0, st[U0], s)
                st[U0] = s
                (rv,) = couple([st[D2] * s + st[G]], 6 + i)
                st[U2] = st[D2] * (st[U0] + st[O] - H2 * rv)
                return carry
            lax.fori_loop(0, t + 1, chain, 0)
        return carry
    lax.fori_loop(0, 2, iteration, 0)

    def beta_copy():
        return pltpu.make_async_remote_copy(src_ref=st.at[M], dst_ref=got.at[2], send_sem=end_send.at[0],
                                            recv_sem=got_sem.at[2], device_id=owner, device_id_type=MESH)

    @pl.when(apart)
    def _():
        beta_copy().start()

    @pl.when(jnp.logical_not(apart))
    def _():
        got[2] = st[M]

    (rg,) = couple([st[G]], 13 + t)
    bs[0] = st[D2] * (st[O] - H2 * rg)

    def b_copy():
        return pltpu.make_async_remote_copy(src_ref=bs.at[0], dst_ref=bs.at[t], send_sem=b_send.at[0],
                                            recv_sem=b_recv.at[t], device_id=worker(0, ex, ey), device_id_type=MESH)

    @pl.when(jnp.logical_not(root))
    def _():
        b_copy().start()

    def r_copy(k, place):
        return pltpu.make_async_remote_copy(src_ref=rh.at[k], dst_ref=got.at[place], send_sem=r_send.at[k],
                                            recv_sem=got_sem.at[place],
                                            device_id={"tm": jnp.minimum(k + 1, NT - 1), "sx": ex, "sy": ey},
                                            device_id_type=MESH)

    @pl.when(root)
    def _():
        def step(k, carry):
            r = jnp.where(k == 0, inp[0:NODES], rh[jnp.maximum(k - 1, 0)])
            (rv,) = couple([st[D2] * r], 14 + k)
            r = jnp.where(k == 0, inp[0:NODES], rh[jnp.maximum(k - 1, 0)])
            ahead = st[D2] * (r - H2 * rv)

            @pl.when(k > 0)
            def _():
                pltpu.make_async_remote_copy(src_ref=bs.at[0], dst_ref=bs.at[k], send_sem=b_send.at[0],
                                             recv_sem=b_recv.at[k], device_id=worker(k, ex, ey),
                                             device_id_type=MESH).wait_recv()
            rh[k] = ahead + bs[k]

            @pl.when(k < NT - 1)
            def _():
                r_copy(k, 0).start()

            @pl.when(k == NT - 1)
            def _():
                r_copy(k, 1).start()
            return carry
        lax.fori_loop(0, NT, step, 0)

    def emit(node, value):
        for f, x in enumerate(fields_of(value)):
            out[0, node, 0, 0, f] = x

    @pl.when(apart)
    def _():
        beta_copy().wait_recv()

    def hand_on():
        return pltpu.make_async_remote_copy(src_ref=got.at[0], dst_ref=got.at[1], send_sem=end_send.at[1],
                                            recv_sem=got_sem.at[1], device_id={"tm": tm - 1, "sx": sx, "sy": sy},
                                            device_id_type=MESH)

    @pl.when(tm > 0)
    def _():
        r_copy(0, 0).wait_recv()
        hand_on().start()
    first = exact(basis_t, got[0])
    emit(0, first)
    st[TMP] = exact(basis_t, got[2]) + 0.5 * first
    r_copy(0, 1).wait_recv()
    last = exact(basis_t, got[1])
    emit(2, last)
    emit(1, st[TMP] + 0.5 * last)

    @pl.when(apart)
    def _():
        beta_copy().wait_send()

    @pl.when(tm > 0)
    def _():
        hand_on().wait_send()

    @pl.when(jnp.logical_not(root))
    def _():
        b_copy().wait_send()

    @pl.when(root)
    def _():
        def done(k, carry):
            r_copy(k, 0).wait_send()
            return carry
        lax.fori_loop(0, NT, done, 0)


def local(initial, viscosity, flux_jacobian):
    consts = [jnp.asarray(x) for x in tables()]
    vmem = pl.BlockSpec(memory_space=pltpu.VMEM)
    state = (NODES, WIDE)
    return pl.pallas_call(
        kernel,
        out_shape=jax.ShapeDtypeStruct((1, 3, 1, 1, FIELDS, NODES, EZ), F32),
        in_specs=[vmem, vmem, pl.BlockSpec(memory_space=pltpu.SMEM)] + [vmem] * 7,
        out_specs=vmem,
        scratch_shapes=[
            pltpu.VMEM((NODES + 8, WIDE), F32),
            pltpu.VMEM((NODES + 8, WIDE), F32),
            pltpu.VMEM((4, 32, WIDE), F32),
            pltpu.VMEM((2, 4, 32, WIDE), F32),
            pltpu.VMEM((18,) + state, F32),
            pltpu.VMEM((NT,) + state, F32),
            pltpu.VMEM((NT,) + state, F32),
            pltpu.VMEM((3,) + state, F32),
            pltpu.SemaphoreType.DMA((2,)),
            pltpu.SemaphoreType.DMA((4,)),
            pltpu.SemaphoreType.DMA((2, 4)),
            pltpu.SemaphoreType.DMA((1,)),
            pltpu.SemaphoreType.DMA((NT,)),
            pltpu.SemaphoreType.DMA((NT,)),
            pltpu.SemaphoreType.DMA((3,)),
            pltpu.SemaphoreType.DMA((2,)),
        ],
        compiler_params=pltpu.CompilerParams(collective_id=0, has_side_effects=True, vmem_limit_bytes=40 << 20),
    )(initial, viscosity, flux_jacobian, *consts)


def solution(mesh):
    return jax.shard_map(
        local,
        mesh=mesh,
        in_specs=(P("sx", "sy", None, None, None), P("sx", "sy", None), P()),
        out_specs=P("tm", None, "sx", "sy", None, None, None),
        check_vma=False,
    )
```

time: 1210 us -> 188 us (0.16)
  the two profiles are of different devices: /device:TPU:9 before, /device:TPU:96 now
where the time goes in v1:
time: 188 us; the launch traced here: 186 us
  Pallas kernels  179 us (95%)
  local copies, waits for them, and re-layouts  7.12 us (4%)
    pallas_call x1, Pallas kernels, local(): pl.pallas_call(kernel, out_shape=jax.ShapeDtypeStruct((1, 3, 1, 1, FIELDS...  179 us
    unnamed x20, local copies, waits for them, and re-layouts  7.12 us

profile of v1, /device:TPU:96, one launch (start us, length us, event | category | flops | bytes accessed | tf_op | source)
XLA Modules:
  0.0 186.4 jit_solution(4041549152897310326)
XLA Ops:
  0.0 0.0 copy-start.2
  0.0 0.0 copy-start.8
  0.0 0.7 copy.11.jac
  0.7 0.1 copy-done.2
  0.8 0.0 copy-done.8
  0.8 0.0 copy-start
  0.8 0.9 copy-done
  1.7 0.0 copy-start.1
  1.7 0.9 copy-done.1
  2.6 0.0 copy-start.3
  2.6 0.8 copy-done.3
  3.4 0.0 copy-start.4
  3.4 0.8 copy-done.4
  4.1 0.0 copy-start.5
  4.1 0.8 copy-done.5
  4.9 0.0 copy-start.6
  4.9 0.8 copy-done.6
  5.6 0.0 copy-start.7
  5.6 0.7 copy-done.7
  6.3 179.2 %shard_map.100 = f32[1,3,1,1,5,64,128]{6,5,4,3,2,1,0:T(8,128)S(1)} custom-call(f32[1,1,5,64,128]{4,3,2,1,0:T(8,128)S(1)} %copy-done, f32[1,1,128]{2,1,0:T(1,128)S(1)} %copy-done.8, f32[3,5,5]{2,1,0:T(8,128)S(1)} %copy.11.jac, bf16[64,192]{1,0:T(8,128)(2,1)S(1)} %copy-done.6, bf16[224,192]{1,0:T(8,128)(2,1)S(1)} %copy-done.1, bf16[64,192]{1,0:T(8,128)(2,1)S(1)} %copy-done.5, ...), custom_call_target="tpu_custom_call" | custom-call | tf_op jit(solution)/shard_map/pallas_call | solution.py:386
  185.6 0.8 copy.13
Async XLA Ops:
  0.0 0.8 copy-start.2
  0.0 0.8 copy-start.8
  0.8 0.9 copy-start
  1.7 0.9 copy-start.1
  2.6 0.8 copy-start.3
  3.4 0.8 copy-start.4
  4.1 0.8 copy-start.5
  4.9 0.8 copy-start.6
  5.6 0.7 copy-start.7

commit v2 on v1

--- a/solution.py
+++ b/solution.py
@@ -57,7 +57,7 @@
 
 
 def worker(t, ex, ey):
-    return {"tm": ex // 2 * 4 + t % 4, "sx": t // 4 * 2 + ex % 2, "sy": ey}
+    return {"tm": (ex // 2 + t) % 4 * 4 + t % 4, "sx": t // 4 * 2 + ex % 2, "sy": ey}
 
 
 def wide(x):
@@ -78,19 +78,27 @@
     return jnp.dot(table[...], x, preferred_element_type=F32, precision=lax.Precision.HIGHEST)
 
 
-def kernel(initial, viscosity, jac, faces_t, local_t, inject_t, inject_z, basis, basis_t, spectrum, out,
-           own, inp, send, recv, st, bs, rh, got,
-           in_sem, send_sem, recv_sem, b_send, b_recv, r_send, got_sem, end_send):
+def kernel(initial_far, viscosity, jac, *refs):
+    far, out = refs[:7], refs[7]
+    near = refs[8:16]
+    initial, faces_t, local_t, inject_t, inject_z, basis, basis_t, spectrum = near
+    (own, inp, own_c, inp_c, send, recv, st, bs, rh, got,
+     load_sem, in_sem, send_sem, recv_sem, b_send, b_recv, r_send, got_sem, end_send) = refs[16:]
+    loads = [pltpu.make_async_copy(a, b, load_sem.at[i]) for i, (a, b) in enumerate(zip((initial_far,) + far, near))]
+    for load in loads:
+        load.start()
     tm, sx, sy = lax.axis_index("tm"), lax.axis_index("sx"), lax.axis_index("sy")
     t = sx // 2 * 4 + tm % 4
-    ex = tm // 4 * 2 + sx % 2
+    ex = (tm // 4 + 4 - tm % 4) % 4 * 2 + sx % 2
     ey = sy
     root = t == 0
-    target = {"tm": sx // 2 * 4 + tm // 4, "sx": tm % 4 * 2 + sx % 2, "sy": sy}
-    source = {"tm": tm % 4 * 4 + sx // 2, "sx": tm // 4 * 2 + sx % 2, "sy": sy}
-    moved = jnp.logical_not(jnp.logical_and(tm // 4 == sx // 2, tm % 4 == sx // 2))
+    kept = (tm // 4 + 4 - sx // 2) % 4
+    target = {"tm": tm // 4 * 4 + kept, "sx": (tm % 4 + 4 - kept + sx // 2) % 4 * 2 + sx % 2, "sy": sy}
+    source = {"tm": tm // 4 * 4 + (tm % 4 + sx // 2 + 4 - ex // 2) % 4, "sx": ex, "sy": sy}
+    moved = ex != sx
     owner = {"tm": t, "sx": ex, "sy": ey}
-    apart = tm // 4 != sx // 2
+    maker = worker(tm, sx, sy)
+    apart = jnp.logical_not(jnp.logical_and(t == tm, ex == sx))
     around = [
         (worker(t, ex - 1, ey), ex > 0, 0),
         (worker(t, ex + 1, ey), ex < NX - 1, 1),
@@ -121,7 +129,7 @@
 
     @pl.when(apart)
     def _():
-        greet(owner)
+        greet(maker)
 
     @pl.when(tm > 0)
     def _():
@@ -138,40 +146,46 @@
             return carry
         lax.fori_loop(1, NT, one, 0)
 
+    for load in loads:
+        load.wait()
     nodal = jnp.concatenate([initial[0, 0, f] for f in range(FIELDS)], axis=1)
-    own[0:NODES] = exact(basis, nodal)
-    own[NODES:NODES + 8] = wide(jnp.broadcast_to(viscosity[0], (8, EZ)))
+    own[...] = exact(basis, nodal)
+    own_c[...] = jnp.broadcast_to(viscosity[0], (8, EZ))
 
     expected = jnp.where(root, NT - 1, 1)
     for there in [there for _, there, _ in around] + [moved, apart, tm > 0]:
         expected = expected + jnp.where(there, 1, 0)
     pl.semaphore_wait(barrier, expected)
 
-    def bring():
-        return pltpu.make_async_remote_copy(src_ref=own, dst_ref=inp, send_sem=in_sem.at[0], recv_sem=in_sem.at[1],
+    def bring(src, dst, i):
+        return pltpu.make_async_remote_copy(src_ref=src, dst_ref=dst, send_sem=in_sem.at[i], recv_sem=in_sem.at[i + 1],
                                             device_id=target, device_id_type=MESH)
 
     @pl.when(moved)
     def _():
-        bring().start()
-        bring().wait()
+        pair = [bring(own_c, inp_c, 0), bring(own, inp, 2)]
+        for one in pair:
+            one.start()
+        for one in pair:
+            one.wait()
 
     @pl.when(jnp.logical_not(moved))
     def _():
         inp[...] = own[...]
+        inp_c[...] = own_c[...]
 
     @pl.when(tm == 0)
     def _():
-        got[0] = own[0:NODES]
-
-    c = inp[NODES:NODES + 8, 0:EZ][0:1]
+        got[0] = own[...]
+
+    c = inp_c[0:1]
     cl = c * spectrum[...]
     st[CL] = wide(cl)
     st[D1] = wide(1.0 / (1.0 + H1 * cl))
     st[D2] = wide(1.0 / (1.0 + H2 * cl))
     st[HC] = wide(jnp.broadcast_to(0.5 * c, (NODES, EZ)))
-    st[U0] = inp[0:NODES]
-    st[U2] = inp[0:NODES]
+    st[U0] = inp[...]
+    st[U2] = inp[...]
     st[M] = jnp.zeros((NODES, WIDE), F32)
     st[RM] = jnp.zeros((NODES, WIDE), F32)
     lane = lax.broadcasted_iota(jnp.int32, (16, EZ), 1)
@@ -195,7 +209,7 @@
         shifted = jnp.concatenate([jnp.concatenate(high, axis=1), jnp.concatenate(low, axis=1)], axis=0)
         return jnp.concatenate(transport, axis=1) - st[HC] * apply(inject_z, split(shifted))
 
-    def couple(values, turn):
+    def couple(values, turn, meanwhile=None):
         slot = turn % 2
         rows = 16 * len(values)
         pieces = [split(v) for v in values]
@@ -213,6 +227,8 @@
             @pl.when(there)
             def _(device=device, k=k):
                 copy(device, k, k ^ 1).start()
+        if meanwhile is not None:
+            meanwhile()
         results = [local_part(p) for p in pieces]
         for device, there, k in around:
             @pl.when(there)
@@ -280,6 +296,17 @@
         return carry
     lax.fori_loop(0, 2, iteration, 0)
 
+    (rg,) = couple([st[G]], 13 + t)
+    bs[0] = st[D2] * (st[O] - H2 * rg)
+
+    def b_copy():
+        return pltpu.make_async_remote_copy(src_ref=bs.at[0], dst_ref=bs.at[t], send_sem=b_send.at[0],
+                                            recv_sem=b_recv.at[t], device_id=worker(0, ex, ey), device_id_type=MESH)
+
+    @pl.when(jnp.logical_not(root))
+    def _():
+        b_copy().start()
+
     def beta_copy():
         return pltpu.make_async_remote_copy(src_ref=st.at[M], dst_ref=got.at[2], send_sem=end_send.at[0],
                                             recv_sem=got_sem.at[2], device_id=owner, device_id_type=MESH)
@@ -291,17 +318,6 @@
     @pl.when(jnp.logical_not(apart))
     def _():
         got[2] = st[M]
-
-    (rg,) = couple([st[G]], 13 + t)
-    bs[0] = st[D2] * (st[O] - H2 * rg)
-
-    def b_copy():
-        return pltpu.make_async_remote_copy(src_ref=bs.at[0], dst_ref=bs.at[t], send_sem=b_send.at[0],
-                                            recv_sem=b_recv.at[t], device_id=worker(0, ex, ey), device_id_type=MESH)
-
-    @pl.when(jnp.logical_not(root))
-    def _():
-        b_copy().start()
 
     def r_copy(k, place):
         return pltpu.make_async_remote_copy(src_ref=rh.at[k], dst_ref=got.at[place], send_sem=r_send.at[k],
@@ -312,9 +328,14 @@
     @pl.when(root)
     def _():
         def step(k, carry):
-            r = jnp.where(k == 0, inp[0:NODES], rh[jnp.maximum(k - 1, 0)])
-            (rv,) = couple([st[D2] * r], 14 + k)
-            r = jnp.where(k == 0, inp[0:NODES], rh[jnp.maximum(k - 1, 0)])
+            r = jnp.where(k == 0, inp[...], rh[jnp.maximum(k - 1, 0)])
+
+            def pass_on():
+                @pl.when(k > 0)
+                def _():
+                    r_copy(k - 1, 0).start()
+            (rv,) = couple([st[D2] * r], 14 + k, pass_on)
+            r = jnp.where(k == 0, inp[...], rh[jnp.maximum(k - 1, 0)])
             ahead = st[D2] * (r - H2 * rv)
 
             @pl.when(k > 0)
@@ -323,10 +344,6 @@
                                              recv_sem=b_recv.at[k], device_id=worker(k, ex, ey),
                                              device_id_type=MESH).wait_recv()
             rh[k] = ahead + bs[k]
-
-            @pl.when(k < NT - 1)
-            def _():
-                r_copy(k, 0).start()
 
             @pl.when(k == NT - 1)
             def _():
@@ -367,7 +384,7 @@
     def _():
         hand_on().wait_send()
 
-    @pl.when(jnp.logical_not(root))
+    @pl.when(t > 0)
     def _():
         b_copy().wait_send()
 
@@ -382,22 +399,26 @@
 def local(initial, viscosity, flux_jacobian):
     consts = [jnp.asarray(x) for x in tables()]
     vmem = pl.BlockSpec(memory_space=pltpu.VMEM)
+    far = pl.BlockSpec(memory_space=pltpu.HBM)
     state = (NODES, WIDE)
     return pl.pallas_call(
         kernel,
         out_shape=jax.ShapeDtypeStruct((1, 3, 1, 1, FIELDS, NODES, EZ), F32),
-        in_specs=[vmem, vmem, pl.BlockSpec(memory_space=pltpu.SMEM)] + [vmem] * 7,
+        in_specs=[far, vmem, pl.BlockSpec(memory_space=pltpu.SMEM)] + [far] * 7,
         out_specs=vmem,
-        scratch_shapes=[
-            pltpu.VMEM((NODES + 8, WIDE), F32),
-            pltpu.VMEM((NODES + 8, WIDE), F32),
+        scratch_shapes=[pltpu.VMEM(x.shape, x.dtype) for x in [initial] + consts] + [
+            pltpu.VMEM(state, F32),
+            pltpu.VMEM(state, F32),
+            pltpu.VMEM((8, EZ), F32),
+            pltpu.VMEM((8, EZ), F32),
             pltpu.VMEM((4, 32, WIDE), F32),
             pltpu.VMEM((2, 4, 32, WIDE), F32),
             pltpu.VMEM((18,) + state, F32),
             pltpu.VMEM((NT,) + state, F32),
             pltpu.VMEM((NT,) + state, F32),
             pltpu.VMEM((3,) + state, F32),
-            pltpu.SemaphoreType.DMA((2,)),
+            pltpu.SemaphoreType.DMA((8,)),
+            pltpu.SemaphoreType.DMA((4,)),
             pltpu.SemaphoreType.DMA((4,)),
             pltpu.SemaphoreType.DMA((2, 4)),
             pltpu.SemaphoreType.DMA((1,)),
@@ -406,7 +427,7 @@
             pltpu.SemaphoreType.DMA((3,)),
             pltpu.SemaphoreType.DMA((2,)),
         ],
-        compiler_params=pltpu.CompilerParams(collective_id=0, has_side_effects=True, vmem_limit_bytes=40 << 20),
+        compiler_params=pltpu.CompilerParams(collective_id=0, has_side_effects=True, vmem_limit_bytes=60 << 20),
     )(initial, viscosity, flux_jacobian, *consts)
 
 

time: 188 us -> 183 us (0.973)
  local copies, waits for them, and re-layouts: 7.12 us -> 3.16 us
    unnamed x20 -> x2, local copies, waits for them, and re-layouts: 7.12 us -> 3.16 us
where the time goes in v2:
time: 183 us
  Pallas kernels  180 us (98%)
  local copies, waits for them, and re-layouts  3.16 us (2%)
    pallas_call x1, Pallas kernels, local(): pl.pallas_call(kernel, out_shape=jax.ShapeDtypeStruct((1, 3, 1, 1, FIELDS...  180 us

profile of v2, /device:TPU:96, one launch (start us, length us, event | category | flops | bytes accessed | tf_op | source)
XLA Modules:
  0.0 183.0 jit_solution(3066691918799386032)
XLA Ops:
  0.0 1.3 copy.11.jac
  1.3 179.8 %shard_map.100 = f32[1,3,1,1,5,64,128]{6,5,4,3,2,1,0:T(8,128)} custom-call(f32[1,1,5,64,128]{4,3,2,1,0:T(8,128)} %initial_far.1, f32[1,1,128]{2,1,0:T(1,128)} %viscosity.1, f32[3,5,5]{2,1,0:T(8,128)} %copy.11.jac, bf16[64,192]{1,0:T(8,128)(2,1)} %constant.14.clone.refs_0_, bf16[224,192]{1,0:T(8,128)(2,1)} %constant.15.clone.refs_1_, ...), custom_call_target="tpu_custom_call" | custom-call | tf_op jit(solution)/shard_map/pallas_call | solution.py:404
  181.2 1.9 %copy.13 = f32[1,3,1,1,5,64,128]{6,5,4,3,2,1,0:T(8,128)} copy(f32[1,3,1,1,5,64,128]{6,5,4,3,2,1,0:T(8,128)} %shard_map.100) | data formatting | bytes 983040

commit v3 on v2

--- a/solution.py
+++ b/solution.py
@@ -105,7 +105,7 @@
         (worker(t, ex, ey - 1), ey > 0, 2),
         (worker(t, ex, ey + 1), ey < NY - 1, 3),
     ]
-    (D1, D2, CL, HC, U0, U2, M, RM, T0, E1, RU0, RU2, U1N, RU1N, O, G, K0, TMP) = range(18)
+    (D1, D2, CL, HC, U0, U2, M, RM, T0, E1, RU0, RU2, U1N, RU1N, O, G, K0, TMP, W2) = range(19)
 
     for _, there, side in around:
         @pl.when(jnp.logical_not(there))
@@ -184,6 +184,7 @@
     st[D1] = wide(1.0 / (1.0 + H1 * cl))
     st[D2] = wide(1.0 / (1.0 + H2 * cl))
     st[HC] = wide(jnp.broadcast_to(0.5 * c, (NODES, EZ)))
+    st[W2] = H2 * st[D2] * st[HC]
     st[U0] = inp[...]
     st[U2] = inp[...]
     st[M] = jnp.zeros((NODES, WIDE), F32)
@@ -209,7 +210,7 @@
         shifted = jnp.concatenate([jnp.concatenate(high, axis=1), jnp.concatenate(low, axis=1)], axis=0)
         return jnp.concatenate(transport, axis=1) - st[HC] * apply(inject_z, split(shifted))
 
-    def couple(values, turn, meanwhile=None):
+    def couple(values, turn, meanwhile=None, fold=None):
         slot = turn % 2
         rows = 16 * len(values)
         pieces = [split(v) for v in values]
@@ -230,6 +231,8 @@
         if meanwhile is not None:
             meanwhile()
         results = [local_part(p) for p in pieces]
+        if fold is not None:
+            st[TMP] = fold(results[0])
         for device, there, k in around:
             @pl.when(there)
             def _(device=device, k=k):
@@ -240,7 +243,8 @@
                 copy(device, k, k ^ 1).wait_send()
         for i in range(len(values)):
             came = jnp.concatenate([recv[slot, k, 16 * i:16 * i + 16] for k in range(4)], axis=0)
-            results[i] = results[i] - st[HC] * apply(inject_t, split(came))
+            gained = apply(inject_t, split(came))
+            results[i] = results[i] - st[HC] * gained if fold is None else st[TMP] + st[W2] * gained
         return results
 
     def sweep(turn_of):
@@ -289,8 +293,7 @@
                 s = st[U2] * 1.0
                 s = jnp.where(i == 0, st[U0], s)
                 st[U0] = s
-                (rv,) = couple([st[D2] * s + st[G]], 6 + i)
-                st[U2] = st[D2] * (st[U0] + st[O] - H2 * rv)
+                (st[U2],) = couple([st[D2] * s + st[G]], 6 + i, None, lambda x: st[D2] * (st[U0] + st[O] - H2 * x))
                 return carry
             lax.fori_loop(0, t + 1, chain, 0)
         return carry
@@ -334,9 +337,7 @@
                 @pl.when(k > 0)
                 def _():
                     r_copy(k - 1, 0).start()
-            (rv,) = couple([st[D2] * r], 14 + k, pass_on)
-            r = jnp.where(k == 0, inp[...], rh[jnp.maximum(k - 1, 0)])
-            ahead = st[D2] * (r - H2 * rv)
+            (ahead,) = couple([st[D2] * r], 14 + k, pass_on, lambda x: st[D2] * (r - H2 * x))
 
             @pl.when(k > 0)
             def _():
@@ -413,7 +414,7 @@
             pltpu.VMEM((8, EZ), F32),
             pltpu.VMEM((4, 32, WIDE), F32),
             pltpu.VMEM((2, 4, 32, WIDE), F32),
-            pltpu.VMEM((18,) + state, F32),
+            pltpu.VMEM((19,) + state, F32),
             pltpu.VMEM((NT,) + state, F32),
             pltpu.VMEM((NT,) + state, F32),
             pltpu.VMEM((3,) + state, F32),

time: 183 us -> 183 us (level)
  no operation moved by 1% of the time
where the time goes in v3:
time: 183 us
  Pallas kernels  180 us (98%)
  local copies, waits for them, and re-layouts  3.16 us (2%)
    pallas_call x1, Pallas kernels, local(): pl.pallas_call(kernel, out_shape=jax.ShapeDtypeStruct((1, 3, 1, 1, FIELDS...  180 us

profile of v3, /device:TPU:96, one launch (start us, length us, event | category | flops | bytes accessed | tf_op | source)
XLA Modules:
  0.0 183.0 jit_solution(14313205896287648863)
XLA Ops:
  0.0 1.3 copy.11.jac
  1.3 179.8 %shard_map.100 = f32[1,3,1,1,5,64,128]{6,5,4,3,2,1,0:T(8,128)} custom-call(f32[1,1,5,64,128]{4,3,2,1,0:T(8,128)} %initial_far.1, f32[1,1,128]{2,1,0:T(1,128)} %viscosity.1, f32[3,5,5]{2,1,0:T(8,128)} %copy.11.jac, bf16[64,192]{1,0:T(8,128)(2,1)} %constant.14.clone.refs_0_, bf16[224,192]{1,0:T(8,128)(2,1)} %constant.15.clone.refs_1_, ...), custom_call_target="tpu_custom_call" | custom-call | tf_op jit(solution)/shard_map/pallas_call | solution.py:405
  181.1 1.9 %copy.13 = f32[1,3,1,1,5,64,128]{6,5,4,3,2,1,0:T(8,128)} copy(f32[1,3,1,1,5,64,128]{6,5,4,3,2,1,0:T(8,128)} %shard_map.100) | data formatting | bytes 983040
